TPU v7x, 32 devices: a whole 2x2x4 slice. The times are simulated.
32 devices in a mesh: leaf: 2 (over x), rows: 16 (over z, y, core).
Axes of the slice: x: 2, y: 2, z: 4, core: 2. Of those that a mesh axis runs over, the one named last changes fastest.
Arguments:
- features: bfloat16 [262144, 256], P(('leaf', 'rows')), parts along dimension 0, may hold values from -80 to 80
- node_ids: int32 [262144], P(('leaf', 'rows')), parts along dimension 0, may hold values from -1 to 15, as said below
- labels: int32 [262144], P(('leaf', 'rows')), parts along dimension 0, may hold values from 0 to 15
- owners: int32 [32], P('leaf'), parts along dimension 0, may hold values from 0 to 15, each once
Outputs:
- hyperplanes: float32 [32, 16, 256], P(('leaf', 'rows')), parts along dimension 0
- scores: float32 [16, 262144], P(None, ('leaf', 'rows')), parts along dimension 1
There are 2 independent parts, one for each index of `leaf`. A program takes and returns all parts, laid end to end along the dimension named above; each array names one. Nothing has to cross between parts.
Inputs may be any that keep to these rules, and one draw needn't show every extreme that they name: `node_ids`: on rows device d, row p of node n's segment (local row n * 512 + p) holds n or -1; the live rows of a segment come first and there is at least one; some segment of every device is full. Each node number appears once in owners; node n is owned by the device of rows with index owners[n].
All inputs are finite; a program needn't handle non-finite values.
Results may differ from a plain program's by a relative error of at most 0.0035.
Values may be sent and summed in bfloat16 or wider, within the bound.
A program may use at most 128 MiB of HBM per device.

v0:
```python
import jax
import jax.numpy as jnp
from jax import lax
from jax.sharding import PartitionSpec as P

CLASSES = 16
ridge_term = 0.1


def solve_nodes(scatter, sums, counts):
    totals = jnp.sum(counts, axis=1)
    centers = jnp.sum(sums, axis=1) / totals[:, None]
    scaled = sums / jnp.maximum(counts, 1.0)[:, :, None]
    within = scatter - jnp.einsum("ncf,ncg->nfg", scaled, sums, precision=lax.Precision.HIGHEST)
    identity = jnp.eye(scatter.shape[-1], dtype=jnp.float32)
    system = within / totals[:, None, None] + ridge_term * identity
    shifts = (sums - counts[:, :, None] * centers[:, None, :]) / totals[:, None, None]
    factor = jnp.linalg.cholesky(system)
    planes = jax.vmap(lambda lower, right: jax.scipy.linalg.cho_solve((lower, True), right.T).T)(
        factor, shifts
    )
    offsets = -jnp.einsum("ncf,nf->nc", planes, centers, precision=lax.Precision.HIGHEST)
    return (planes, offsets)


def on_device(features, node_ids, labels, owners):
    row_count, feature_count = features.shape
    node_count = owners.shape[0]
    segment = row_count // node_count
    inverse = (
        jnp.zeros((node_count,), jnp.int32).at[owners].set(jnp.arange(node_count, dtype=jnp.int32))
    )
    blocks = jnp.take(features.reshape(node_count, segment, feature_count), inverse, axis=0)
    slot_ids = jnp.take(node_ids.reshape(node_count, segment), inverse, axis=0)
    marks = jnp.take(labels.reshape(node_count, segment), inverse, axis=0)
    live_rows = slot_ids == inverse[:, None]
    masked = jnp.where(live_rows[:, :, None], blocks, jnp.zeros((), jnp.bfloat16))
    classes = jnp.arange(CLASSES, dtype=jnp.int32)
    tagged = jnp.where(live_rows, marks, -1).astype(jnp.bfloat16)
    arrived, arrived_tags = (
        lax.all_to_all(masked, "rows", split_axis=0, concat_axis=1, tiled=True),
        lax.all_to_all(tagged, "rows", split_axis=0, concat_axis=1, tiled=True),
    )
    owner_tags = arrived_tags.astype(jnp.int32)
    owner_hot = (owner_tags[:, None, :] == classes[None, :, None]).astype(jnp.bfloat16)
    mine_sums = jnp.einsum("ncs,nsf->ncf", owner_hot, arrived, preferred_element_type=jnp.float32)
    mine_counts = jnp.sum(owner_hot.astype(jnp.float32), axis=2)
    scatter = jnp.einsum("nsf,nsg->nfg", arrived, arrived, preferred_element_type=jnp.float32)
    planes, offsets = solve_nodes(scatter, mine_sums, mine_counts)
    every_planes, every_offsets = (
        lax.all_gather(planes, "rows", axis=0, tiled=True),
        lax.all_gather(offsets, "rows", axis=0, tiled=True),
    )
    rounded = every_planes.astype(jnp.bfloat16)
    result = jnp.einsum("ncf,nsf->cns", rounded, blocks, preferred_element_type=jnp.float32)
    result = result + every_offsets.T[:, :, None]
    result = jnp.where(live_rows[None], result, 0.0)
    result = jnp.take(result, owners, axis=1).reshape(CLASSES, row_count)
    return (planes, result)


def solution(mesh):
    in_specs = (P(("leaf", "rows"), None), P(("leaf", "rows")), P(("leaf", "rows")), P("leaf"))
    out_specs = (P(("leaf", "rows"), None, None), P(None, ("leaf", "rows")))
    return jax.shard_map(
        on_device, mesh=mesh, in_specs=in_specs, out_specs=out_specs, check_vma=False
    )
```

profile of v0, /device:TPU:0, one launch (start us, length us, event | category | flops | bytes accessed | tf_op | source)
XLA Modules:
  0.0 252.2 jit_solution(4196847479306877663)
XLA Ops:
  1.9 0.7 compare_and_fusion
  2.6 0.8 reshape.307
  3.4 0.8 reshape.309
  7.2 7.4 %all-to-all-start.1 = ((bf16[16,2,256]{2,1,0:T(2,128)(2,1)}), bf16[16,2,256]{2,1,0:T(2,128)(2,1)S(1)}, u32[]{:S(2)}, u32[]{:S(2)}) async-start(bf16[16,2,256]{2,1,0:T(2,128)(2,1)} %reshape.402), calls=%async_computation.1 | async-start | bytes 32768 | tf_op jit(solution)/shard_map/all_to_all | solution.py:42
  14.6 4.9 %gather_fusion = bf16[16,512,256]{2,1,0:T(8,128)(2,1)} fusion(bf16[16,512,256]{2,1,0:T(8,128)(2,1)} %bitcast.110, s32[1024]{0:T(1024)S(1)} %pad_clamp_fusion.1), kind=kCustom, calls=%fused_computation.2 | custom fusion | bytes 8388672 | tf_op jit(solution)/shard_map/jit(_take)/gather | solution.py:33
  19.5 5.3 %broadcast_select_fusion.1 = bf16[16,512,256]{2,1,0:T(8,128)(2,1)} fusion(pred[16,512]{1,0:T(8,128)(4,1)S(1)} %get-tuple-element.24, bf16[16,512,256]{2,1,0:T(8,128)(2,1)} %gather_fusion, pred[16]{0:T(512)(128)(4,1)S(1)} %get-tuple-element.35), kind=kLoop, calls=%fused_computation.8 | loop fusion | flops 4194304 | bytes 8396816 | tf_op jit(solution)/shard_map/jit(_where)/select_n | solution.py:37
  24.8 6.2 %all-to-all-start = ((bf16[16,512,256]{2,1,0:T(8,128)(2,1)}), bf16[16,512,256]{2,1,0:T(8,128)(2,1)}, u32[]{:S(2)}, u32[]{:S(2)}) async-start(bf16[16,512,256]{2,1,0:T(8,128)(2,1)} %broadcast_select_fusion.1), calls=%async_computation | async-start | bytes 8388608 | tf_op jit(solution)/shard_map/all_to_all | solution.py:41
  32.5 0.8 convert_reduce_fusion.1
  33.2 75.3 %all-to-all-done = bf16[16,512,256]{2,1,0:T(8,128)(2,1)} async-done(((bf16[16,512,256]{2,1,0:T(8,128)(2,1)}), bf16[16,512,256]{2,1,0:T(8,128)(2,1)}, u32[]{:S(2)}, u32[]{:S(2)}) %all-to-all-start) | async-done | bytes 4194336 | tf_op jit(solution)/shard_map/all_to_all | solution.py:41
  108.5 2.9 %fusion.33 = (f32[256]{0:T(256)S(1)}, f32[16,256]{1,0:T(8,128)S(1)}) fusion(bf16[8192,256]{1,0:T(8,128)(2,1)} %bitcast.4, s32[8192]{0:T(1024)S(1)} %bitcast.115), kind=kOutput, calls=%fused_computation.85 | convolution fusion | flops 67243776 | bytes 4244480 | tf_op jit(solution)/shard_map/ncs,nsf->ncf/dot_general | solution.py:46
  112.1 0.7 divide_bitcast_fusion
  112.8 5.2 %convolution_bitcast_fusion = f32[256,256]{0,1:T(8,128)S(1)} fusion(bf16[16,512,256]{2,1,0:T(8,128)(2,1)} %all-to-all-done), kind=kOutput, calls=%fused_computation.16 | convolution fusion | flops 1073741824 | bytes 4456448 | tf_op jit(solution)/shard_map/nsf,nsg->nfg/dot_general | solution.py:48
  118.0 1.1 fusion.5
  119.3 11.7 %custom-call.20 = f32[1,128,128]{2,1,0:T(8,128)S(1)} custom-call(f32[1,128,128]{2,1,0:T(8,128)S(1)} %cholesky.117), custom_call_target="Cholesky" | custom-call | tf_op jit(solution)/shard_map/jit(cholesky)/cholesky | solution.py:18
  131.0 9.8 %custom-call.21 = f32[1,1,128,128]{2,3,1,0:T(8,128)S(1)} custom-call(f32[1,1,128,128]{3,2,1,0:T(8,128)S(1)} %get-tuple-element.30), custom_call_target="InvertDiagBlocksLowerTriangular" | custom-call | tf_op jit(solution)/shard_map/jit(cholesky)/cholesky | solution.py:18
  141.3 11.9 %custom-call.22 = f32[1,128,128]{2,1,0:T(8,128)S(1)} custom-call(f32[1,128,128]{2,1,0:T(8,128)S(1)} %fusion.6), custom_call_target="Cholesky" | custom-call | tf_op jit(solution)/shard_map/jit(cholesky)/cholesky | solution.py:18
  155.9 3.9 %while.1 = (s32[]{:T(128)}, f32[1,256,256]{2,1,0:T(8,128)S(1)}, s32[2,2]{1,0:T(2,128)S(1)}, f32[2,1,128,128]{3,2,1,0:T(8,128)S(1)}, s32[]{:T(128)}) while((s32[]{:T(128)}, f32[1,256,256]{2,1,0:T(8,128)S(1)}, s32[2,2]{1,0:T(2,128)S(1)}, f32[2,1,128,128]{3,2,1,0:T(8,128)S(1)}, s32[]{:T(128)}) %tuple.32), condition=%wide.while_cond, body=%wide.while_body.sunk | while | flops 2 | bytes 131181 | solution.py:19
  156.5 1.4 bitcast_dynamic-update-slice_fusion.3
  158.5 1.4 bitcast_dynamic-update-slice_fusion.3
  159.9 19.7 %custom-call.23 = f32[1,2,128,128]{2,3,1,0:T(8,128)S(1)} custom-call(f32[1,2,128,128]{3,2,1,0:T(8,128)S(1)} %bitcast.121), custom_call_target="InvertDiagBlocksLowerTriangular" | custom-call | tf_op jit(solution)/shard_map/vmap(jit(_cho_solve))/triangular_solve | solution.py:19
  181.3 35.7 %all_gather.6 = bf16[16,16,256]{2,1,0:T(8,128)(2,1)S(1)} all-gather(bf16[1,16,256]{2,1,0:T(8,128)(2,1)S(1)} %get-tuple-element.21), channel_id=1, replica_groups=mesh['leaf'=2,'rows'=16] {'rows'}, dimensions={0}, use_global_device_ids=true | all-gather | bytes 139264 | tf_op jit(solution)/shard_map/all_gather | solution.py:51
  217.4 29.8 %all-reduce.1 = f32[256]{0:T(256)S(1)} all-reduce(f32[256]{0:T(256)S(1)} %dynamic-update-slice.11), channel_id=2, replica_groups=mesh['leaf'=2,'rows'=16] {'rows'}, use_global_device_ids=true, to_apply=%add.1 | all-reduce | flops 256 | bytes 2048
  247.2 3.4 %fusion.3 = f32[16,16,512]{2,0,1:T(8,128)S(1)} fusion(bf16[16,512,256]{2,1,0:T(8,128)(2,1)} %gather_fusion, pred[16]{0:T(512)(128)(4,1)S(1)} %get-tuple-element.35, f32[16,16]{0,1:T(8,128)S(1)} %bitcast.120, pred[16,512]{1,0:T(8,128)(4,1)S(1)} %get-tuple-element.24, bf16[16,16,256]{2,1,0:T(8,128)(2,1)S(1)} %all_gather.6), kind=kOutput, calls=%fused_computation.12 | convolution fusion | flops 69468160 | bytes 4858896 | tf_op jit(solution)/shard_map/ncf,nsf->cns/dot_general | solution.py:55
  251.4 0.8 broadcast_select_fusion.9
  (53 shorter events, 11.9 us)
Async XLA Ops:
  7.2 17.6 %all-to-all-start.1 = ((bf16[16,2,256]{2,1,0:T(2,128)(2,1)}), bf16[16,2,256]{2,1,0:T(2,128)(2,1)S(1)}, u32[]{:S(2)}, u32[]{:S(2)}) async-start(bf16[16,2,256]{2,1,0:T(2,128)(2,1)} %reshape.402), calls=%async_computation.1 | async-start | bytes 32768 | tf_op jit(solution)/shard_map/all_to_all | solution.py:42
  24.8 6.3 %copy-start = (u32[32]{0:T(128)S(1)}, u32[32]{0:T(128)}, u32[]{:S(2)}) copy-start(u32[32]{0:T(128)} %constant.166) | copy-start | bytes 388
  24.8 83.7 %all-to-all-start = ((bf16[16,512,256]{2,1,0:T(8,128)(2,1)}), bf16[16,512,256]{2,1,0:T(8,128)(2,1)}, u32[]{:S(2)}, u32[]{:S(2)}) async-start(bf16[16,512,256]{2,1,0:T(8,128)(2,1)} %broadcast_select_fusion.1), calls=%async_computation | async-start | bytes 8388608 | tf_op jit(solution)/shard_map/all_to_all | solution.py:41
where the time goes:
time: 253 us; the launch traced here: 252 us
  waiting for transfers between devices  75.3 us (30%)
  other arithmetic  65.5 us (26%)
  blocking collectives  65.5 us (26%)
  local copies, waits for them, and re-layouts  15.1 us (6%)
  matrix products  14.3 us (6%)
  starting transfers between devices  13.6 us (5%)
  between operations  2.8 us (1%)
    all_to_all x1, waiting for transfers between devices, on_device(): lax.all_to_all(masked, 'rows', split_axis=0, concat_axis=1, tiled=True)  75.3 us
    all_gather x1, blocking collectives, on_device(): lax.all_gather(planes, 'rows', axis=0, tiled=True)  35.7 us
    another operation x7, other arithmetic, solve_nodes(): factor = jnp.linalg.cholesky(system)  34.8 us
    unnamed x1, blocking collectives  29.8 us
    another operation x3, other arithmetic, solve_nodes(): jax.scipy.linalg.cho_solve((lower, True), right.T)  19.7 us
    all_to_all x1, starting transfers between devices, on_device(): lax.all_to_all(tagged, 'rows', split_axis=0, concat_axis=1, tiled=True)  7.41 us
    all_to_all x1, starting transfers between devices, on_device(): lax.all_to_all(masked, 'rows', split_axis=0, concat_axis=1, tiled=True)  6.19 us
    select_n x1, other arithmetic, on_device(): jnp.where(live_rows[:, :, None], blocks, jnp.zeros((), jnp.bfloat16))  5.27 us
  transfers between devices with their start and end apart: 2, of which 1 were waited for; matrix products, arithmetic and copies ran while one was open for 5% of the time, Pallas kernels for 0%

commit v1 on v0

--- a/solution.py
+++ b/solution.py
@@ -2,6 +2,7 @@
 import jax.numpy as jnp
 from jax import lax
 from jax.sharding import PartitionSpec as P
+from jax.lax import all_to_all, psum
 
 CLASSES = 16
 ridge_term = 0.1
@@ -37,8 +38,12 @@
     masked = jnp.where(live_rows[:, :, None], blocks, jnp.zeros((), jnp.bfloat16))
     classes = jnp.arange(CLASSES, dtype=jnp.int32)
     tagged = jnp.where(live_rows, marks, -1).astype(jnp.bfloat16)
+    handle_the_tokens = lambda field, join_dim, on_dim: jnp.concatenate(
+        all_to_all(jnp.stack(jnp.split(field, psum(1, "rows"), join_dim), axis=0), "rows", 0, 0),
+        on_dim,
+    )
     arrived, arrived_tags = (
-        lax.all_to_all(masked, "rows", split_axis=0, concat_axis=1, tiled=True),
+        handle_the_tokens(masked, 0, 1),
         lax.all_to_all(tagged, "rows", split_axis=0, concat_axis=1, tiled=True),
     )
     owner_tags = arrived_tags.astype(jnp.int32)

time: 253 us -> 263 us (1.040)
  local copies, waits for them, and re-layouts: 15.1 us -> 26.7 us
    unnamed x9 -> x24, local copies, waits for them, and re-layouts: 1.53 us -> 12.4 us
  transfers between devices with their start and end apart: 2 -> 2, of which waited for: 1 -> 1; matrix products, arithmetic and copies ran while one was open for 5% -> 8% of each run, Pallas kernels for 0% -> 0%
where the time goes in v1:
time: 263 us; the launch traced here: 262 us
  waiting for transfers between devices  75.3 us (29%)
  blocking collectives  65.5 us (25%)
  other arithmetic  63.9 us (24%)
  local copies, waits for them, and re-layouts  26.7 us (10%)
  matrix products  14.3 us (5%)
  starting transfers between devices  13.6 us (5%)
  between operations  2.81 us (1%)
    all_to_all x1, waiting for transfers between devices, on_device(): all_to_all(jnp.stack(jnp.split(field, psum(1, 'rows'), join_dim), axis=0)...  75.3 us
    all_gather x1, blocking collectives, on_device(): lax.all_gather(planes, 'rows', axis=0, tiled=True)  35.7 us
    another operation x7, other arithmetic, solve_nodes(): factor = jnp.linalg.cholesky(system)  34.8 us
    unnamed x1, blocking collectives  29.8 us
    another operation x3, other arithmetic, solve_nodes(): jax.scipy.linalg.cho_solve((lower, True), right.T)  19.7 us
    unnamed x24, local copies, waits for them, and re-layouts  12.4 us
    all_to_all x1, starting transfers between devices, on_device(): lax.all_to_all(tagged, 'rows', split_axis=0, concat_axis=1, tiled=True)  7.41 us
    all_to_all x1, starting transfers between devices, on_device(): all_to_all(jnp.stack(jnp.split(field, psum(1, 'rows'), join_dim), axis=0)...  6.19 us
  transfers between devices with their start and end apart: 2, of which 1 were waited for; matrix products, arithmetic and copies ran while one was open for 8% of the time, Pallas kernels for 0%

profile of v1, /device:TPU:0, one launch (start us, length us, event | category | flops | bytes accessed | tf_op | source)
XLA Modules:
  0.0 262.2 jit_solution(5947443666818444721)
XLA Ops:
  2.6 0.8 reshape.309
  3.4 0.8 reshape.312
  7.2 7.4 %all-to-all-start.1 = ((bf16[16,2,256]{2,1,0:T(2,128)(2,1)}), bf16[16,2,256]{2,1,0:T(2,128)(2,1)S(1)}, u32[]{:S(2)}, u32[]{:S(2)}) async-start(bf16[16,2,256]{2,1,0:T(2,128)(2,1)} %reshape.405), calls=%async_computation.1 | async-start | bytes 32768 | tf_op jit(solution)/shard_map/all_to_all | solution.py:47
  14.6 4.9 %gather_fusion = bf16[16,512,256]{2,1,0:T(8,128)(2,1)} fusion(bf16[16,512,256]{2,1,0:T(8,128)(2,1)} %bitcast.177, s32[1024]{0:T(1024)S(1)} %pad_clamp_fusion.1), kind=kCustom, calls=%fused_computation.2 | custom fusion | bytes 8388672 | tf_op jit(solution)/shard_map/jit(_take)/gather | solution.py:34
  19.5 3.6 %broadcast_select_fusion.1 = bf16[16,512,256]{2,1,0:T(8,128)(2,1)S(1)} fusion(pred[16,512]{1,0:T(8,128)(4,1)S(1)} %get-tuple-element.24, bf16[16,512,256]{2,1,0:T(8,128)(2,1)} %gather_fusion, pred[16]{0:T(512)(128)(4,1)S(1)} %get-tuple-element.35), kind=kLoop, calls=%fused_computation.10 | loop fusion | flops 4194304 | bytes 8396816 | tf_op jit(solution)/shard_map/jit(_where)/select_n | solution.py:38
  24.6 0.7 fusion.30
  25.3 0.7 fusion.29
  34.8 6.2 %all-to-all-start = ((bf16[16,1,512,256]{3,2,1,0:T(8,128)(2,1)}), bf16[16,1,512,256]{3,2,1,0:T(8,128)(2,1)}, u32[]{:S(2)}, u32[]{:S(2)}) async-start(bf16[16,1,512,256]{3,2,1,0:T(8,128)(2,1)} %fusion.17), calls=%async_computation | async-start | bytes 8388608 | tf_op jit(solution)/shard_map/all_to_all | solution.py:42
  42.4 0.8 convert_reduce_fusion.1
  43.2 75.3 %all-to-all-done = bf16[16,1,512,256]{3,2,1,0:T(8,128)(2,1)} async-done(((bf16[16,1,512,256]{3,2,1,0:T(8,128)(2,1)}), bf16[16,1,512,256]{3,2,1,0:T(8,128)(2,1)}, u32[]{:S(2)}, u32[]{:S(2)}) %all-to-all-start) | async-done | bytes 4194336 | tf_op jit(solution)/shard_map/all_to_all | solution.py:42
  118.5 2.9 %fusion.54 = (f32[256]{0:T(256)S(1)}, f32[16,256]{1,0:T(8,128)S(1)}) fusion(bf16[8192,256]{1,0:T(8,128)(2,1)} %bitcast.21, s32[8192]{0:T(1024)S(1)} %bitcast.182), kind=kOutput, calls=%fused_computation.119 | convolution fusion | flops 67243776 | bytes 4244480 | tf_op jit(solution)/shard_map/ncs,nsf->ncf/dot_general | solution.py:51
  122.8 5.2 %fusion.8 = f32[256,256]{0,1:T(8,128)S(1)} fusion(bf16[16,1,512,256]{3,2,1,0:T(8,128)(2,1)} %all-to-all-done), kind=kOutput, calls=%fused_computation.18 | convolution fusion | flops 1073741824 | bytes 4456448 | tf_op jit(solution)/shard_map/nsf,nsg->nfg/dot_general | solution.py:53
  128.0 1.1 fusion.7
  129.3 11.7 %custom-call.20 = f32[1,128,128]{2,1,0:T(8,128)S(1)} custom-call(f32[1,128,128]{2,1,0:T(8,128)S(1)} %cholesky.117), custom_call_target="Cholesky" | custom-call | tf_op jit(solution)/shard_map/jit(cholesky)/cholesky | solution.py:19
  141.0 9.8 %custom-call.21 = f32[1,1,128,128]{2,3,1,0:T(8,128)S(1)} custom-call(f32[1,1,128,128]{3,2,1,0:T(8,128)S(1)} %get-tuple-element.30), custom_call_target="InvertDiagBlocksLowerTriangular" | custom-call | tf_op jit(solution)/shard_map/jit(cholesky)/cholesky | solution.py:19
  151.3 11.9 %custom-call.22 = f32[1,128,128]{2,1,0:T(8,128)S(1)} custom-call(f32[1,128,128]{2,1,0:T(8,128)S(1)} %fusion.11), custom_call_target="Cholesky" | custom-call | tf_op jit(solution)/shard_map/jit(cholesky)/cholesky | solution.py:19
  165.9 3.9 %while.1 = (s32[]{:T(128)}, f32[1,256,256]{2,1,0:T(8,128)S(1)}, s32[2,2]{1,0:T(2,128)S(1)}, f32[2,1,128,128]{3,2,1,0:T(8,128)S(1)}, s32[]{:T(128)}) while((s32[]{:T(128)}, f32[1,256,256]{2,1,0:T(8,128)S(1)}, s32[2,2]{1,0:T(2,128)S(1)}, f32[2,1,128,128]{3,2,1,0:T(8,128)S(1)}, s32[]{:T(128)}) %tuple.32), condition=%wide.while_cond, body=%wide.while_body.sunk | while | flops 2 | bytes 131181 | solution.py:20
  166.5 1.4 bitcast_dynamic-update-slice_fusion.3
  168.5 1.4 bitcast_dynamic-update-slice_fusion.3
  169.8 19.7 %custom-call.23 = f32[1,2,128,128]{2,3,1,0:T(8,128)S(1)} custom-call(f32[1,2,128,128]{3,2,1,0:T(8,128)S(1)} %bitcast.188), custom_call_target="InvertDiagBlocksLowerTriangular" | custom-call | tf_op jit(solution)/shard_map/vmap(jit(_cho_solve))/triangular_solve | solution.py:20
  191.3 35.7 %all_gather.6 = bf16[16,16,256]{2,1,0:T(8,128)(2,1)S(1)} all-gather(bf16[1,16,256]{2,1,0:T(8,128)(2,1)S(1)} %get-tuple-element.21), channel_id=1, replica_groups=mesh['leaf'=2,'rows'=16] {'rows'}, dimensions={0}, use_global_device_ids=true | all-gather | bytes 139264 | tf_op jit(solution)/shard_map/all_gather | solution.py:56
  227.3 29.8 %all-reduce.1 = f32[256]{0:T(256)S(1)} all-reduce(f32[256]{0:T(256)S(1)} %dynamic-update-slice.11), channel_id=2, replica_groups=mesh['leaf'=2,'rows'=16] {'rows'}, use_global_device_ids=true, to_apply=%add.1 | all-reduce | flops 256 | bytes 2048
  257.2 3.4 %fusion.5 = f32[16,16,512]{2,0,1:T(8,128)S(1)} fusion(bf16[16,512,256]{2,1,0:T(8,128)(2,1)} %gather_fusion, pred[16]{0:T(512)(128)(4,1)S(1)} %get-tuple-element.35, f32[16,16]{0,1:T(8,128)S(1)} %bitcast.187, pred[16,512]{1,0:T(8,128)(4,1)S(1)} %get-tuple-element.24, bf16[16,16,256]{2,1,0:T(8,128)(2,1)S(1)} %all_gather.6), kind=kOutput, calls=%fused_computation.14 | convolution fusion | flops 69468160 | bytes 4858896 | tf_op jit(solution)/shard_map/ncf,nsf->cns/dot_general | solution.py:60
  261.3 0.8 broadcast_select_fusion.9
  (69 shorter events, 23.4 us)
Async XLA Ops:
  7.2 27.6 %all-to-all-start.1 = ((bf16[16,2,256]{2,1,0:T(2,128)(2,1)}), bf16[16,2,256]{2,1,0:T(2,128)(2,1)S(1)}, u32[]{:S(2)}, u32[]{:S(2)}) async-start(bf16[16,2,256]{2,1,0:T(2,128)(2,1)} %reshape.405), calls=%async_computation.1 | async-start | bytes 32768 | tf_op jit(solution)/shard_map/all_to_all | solution.py:47
  34.8 6.3 %copy-start = (u32[32]{0:T(128)S(1)}, u32[32]{0:T(128)}, u32[]{:S(2)}) copy-start(u32[32]{0:T(128)} %constant.166) | copy-start | bytes 388
  34.8 83.7 %all-to-all-start = ((bf16[16,1,512,256]{3,2,1,0:T(8,128)(2,1)}), bf16[16,1,512,256]{3,2,1,0:T(8,128)(2,1)}, u32[]{:S(2)}, u32[]{:S(2)}) async-start(bf16[16,1,512,256]{3,2,1,0:T(8,128)(2,1)} %fusion.17), calls=%async_computation | async-start | bytes 8388608 | tf_op jit(solution)/shard_map/all_to_all | solution.py:42
